TPU v7x, 128 devices: a whole 4x4x4 slice. The times are simulated.
128 devices in a mesh: dp: 16 (over x, y), tensor: 8 (over z, core).
Axes of the slice: x: 4, y: 4, z: 4, core: 2. Of those that a mesh axis runs over, the one named last changes fastest.
Arguments:
- hidden_rows: bfloat16 [256, 32, 8192], P('tensor', 'dp'), may hold values from -6 to 6
- norm_gain: float32 [8192], replicated, may hold values from 0.1 to 1.9
- w_query: bfloat16 [8192, 4096], P(None, 'tensor'), may hold values from -0.0625 to 0.0625
- w_key: bfloat16 [8192, 1024], P(None, 'tensor'), may hold values from -0.0625 to 0.0625
- w_value: bfloat16 [8192, 1024], P(None, 'tensor'), may hold values from -0.0625 to 0.0625
- w_out: bfloat16 [4096, 8192], P('tensor'), may hold values from -1.5 to 1.5
- cache_keys: bfloat16 [32, 2048, 1024], P('dp', None, 'tensor'), may hold values from -6 to 6
- cache_values: bfloat16 [32, 2048, 1024], P('dp', None, 'tensor'), may hold values from -6 to 6
- slot_of_request: int32 [32], replicated, may hold values from 0 to 31, as said below
- span_length: int32 [32], replicated, may hold values from 1 to 256, as said below
- prefix_length: int32 [32], replicated, may hold values from 1 to 2048, as said below
Outputs:
- attention_out: bfloat16 [256, 32, 8192], P('tensor', 'dp')
Inputs may be any that keep to these rules, and one draw needn't show every extreme that they name: `slot_of_request`: a permutation of the slots 0 to 31; slot i lies on dp index i // 2, request r starts on dp index r // 2; there are 2 distinct numbers m, one of them 1, the same for every dp index, such that the 2 requests of dp index i have their slots on the dp indices i XOR m, one on each. `span_length`: some request uses all 256 new positions. `prefix_length`: some request has all 2048 cached positions.
All inputs are finite; a program needn't handle non-finite values.
Results may differ from a plain program's by a relative error of at most 0.019.
Values may be sent and summed in bfloat16 or wider, within the bound.
A program may use at most 128 MiB of HBM per device.

v0:
```python
import jax
import jax.numpy as jnp
from jax import lax
from jax.sharding import PartitionSpec as P

HD = 128
rope_base = 500000.0
norm_eps = 1e-05
masked = -1e30


def rotate(values, position):
    head_width = values.shape[-1]
    half_width = head_width // 2
    frequency = rope_base ** (-(jnp.arange(half_width, dtype=jnp.float32) * 2.0 / head_width))
    angles = position[..., None, None] * frequency
    cosine = jnp.cos(angles)
    sine_part = jnp.sin(angles)
    front_half = values[..., :half_width]
    back_half = values[..., half_width:]
    return jnp.concatenate(
        [front_half * cosine - back_half * sine_part, back_half * cosine + front_half * sine_part],
        axis=-1,
    )


def normalize(hidden_rows, norm_gain):
    floats = hidden_rows.astype(jnp.float32)
    return (
        floats * lax.rsqrt(jnp.mean(floats * floats, axis=-1, keepdims=True) + norm_eps) * norm_gain
    ).astype(jnp.bfloat16)


def project_group(normed, prefix_here, w_query, w_key, w_value):
    piece_rows = lax.all_gather(normed, "tensor", axis=0, tiled=True)
    row_count = piece_rows.shape[0]
    request_count = piece_rows.shape[1]
    positions = (prefix_here[None, :] + jnp.arange(row_count, dtype=jnp.int32)[:, None]).astype(
        jnp.float32
    )
    queries = jnp.einsum("nsd,df->nsf", piece_rows, w_query, preferred_element_type=jnp.float32)
    queries = rotate(queries.reshape(row_count, request_count, -1, HD), positions)
    keys_new = jnp.einsum("nsd,df->nsf", piece_rows, w_key, preferred_element_type=jnp.float32)
    keys_new = rotate(keys_new.reshape(row_count, request_count, -1, HD), positions)
    values_new = jnp.einsum("nsd,df->nsf", piece_rows, w_value, preferred_element_type=jnp.float32)
    return jnp.concatenate(
        [
            queries.reshape(row_count, request_count, -1).astype(jnp.bfloat16),
            keys_new.reshape(row_count, request_count, -1).astype(jnp.bfloat16),
            values_new.astype(jnp.bfloat16),
        ],
        axis=-1,
    )


def attend_slots(packed, cache_keys, cache_values, slot_prefix, slot_length, q_width, kv_width):
    span_rows = packed.shape[0]
    slot_count = packed.shape[1]
    kv_heads = kv_width // HD
    groups = q_width // kv_width
    prefix = cache_keys.shape[1]
    score_scale = HD ** (-0.5)
    queries = packed[..., :q_width].reshape(span_rows, slot_count, kv_heads, groups, HD)
    keys_new = packed[..., q_width : q_width + kv_width].reshape(
        span_rows, slot_count, kv_heads, HD
    )
    values_new = packed[..., q_width + kv_width :].reshape(span_rows, slot_count, kv_heads, HD)
    keys_old = cache_keys.reshape(slot_count, prefix, kv_heads, HD)
    values_old = cache_values.reshape(slot_count, prefix, kv_heads, HD)
    score_old = (
        jnp.einsum("csgmd,spgd->sgmcp", queries, keys_old, preferred_element_type=jnp.float32)
        * score_scale
    )
    score_new = (
        jnp.einsum("csgmd,jsgd->sgmcj", queries, keys_new, preferred_element_type=jnp.float32)
        * score_scale
    )
    keep_old = jnp.arange(prefix, dtype=jnp.int32)[None, :] < slot_prefix[:, None]
    row_index = jnp.arange(span_rows, dtype=jnp.int32)
    keep_new = (row_index[None, None, :] < slot_length[:, None, None]) & (
        row_index[None, None, :] <= row_index[None, :, None]
    )
    score_old = jnp.where(keep_old[:, None, None, None, :], score_old, masked)
    score_new = jnp.where(keep_new[:, None, None, :, :], score_new, masked)
    exp_old = jnp.exp(score_old)
    exp_new = jnp.exp(score_new)
    denominator = jnp.sum(exp_old, axis=-1, keepdims=True) + jnp.sum(
        exp_new, axis=-1, keepdims=True
    )
    weight_old = (exp_old / denominator).astype(jnp.bfloat16)
    weight_new = (exp_new / denominator).astype(jnp.bfloat16)
    mixed = jnp.einsum(
        "sgmcp,spgd->csgmd", weight_old, values_old, preferred_element_type=jnp.float32
    )
    mixed = mixed + jnp.einsum(
        "sgmcj,jsgd->csgmd", weight_new, values_new, preferred_element_type=jnp.float32
    )
    return mixed.astype(jnp.bfloat16).reshape(span_rows, slot_count, q_width)


def local(
    hidden_rows,
    norm_gain,
    w_query,
    w_key,
    w_value,
    w_out,
    cache_keys,
    cache_values,
    slot_of_request,
    span_length,
    prefix_length,
):
    data_size = lax.axis_size("dp")
    data_index = lax.axis_index("dp")
    per_device = hidden_rows.shape[1]
    q_width = w_query.shape[1]
    kv_width = w_key.shape[1]
    all_requests = slot_of_request.shape[0]
    request_ids = jnp.arange(all_requests, dtype=jnp.int32)
    devices = jnp.arange(data_size, dtype=jnp.int32)
    first_request = data_index * per_device
    my_slots = lax.dynamic_slice_in_dim(slot_of_request, first_request, per_device)
    send_table = (devices[:, None] == my_slots[None, :] // per_device).astype(jnp.bfloat16)
    slot_match = (
        slot_of_request[None, :]
        == (first_request + jnp.arange(per_device, dtype=jnp.int32))[:, None]
    )
    source_match = request_ids[None, :] // per_device == devices[:, None]
    recv_table = jnp.any(slot_match[:, None, :] & source_match[None, :, :], axis=-1).astype(
        jnp.bfloat16
    )
    slot_prefix = jnp.sum(jnp.where(slot_match, prefix_length[None, :], 0), axis=1)
    slot_length = jnp.sum(jnp.where(slot_match, span_length[None, :], 0), axis=1)
    normed = normalize(hidden_rows, norm_gain)
    outgoing = jnp.einsum(
        "js,csf->jcf", send_table, normed, preferred_element_type=jnp.float32
    ).astype(jnp.bfloat16)
    incoming = lax.all_to_all(outgoing, "dp", split_axis=0, concat_axis=0, tiled=True)
    slot_rows = jnp.einsum(
        "sj,jcf->csf", recv_table, incoming, preferred_element_type=jnp.float32
    ).astype(jnp.bfloat16)
    packed = project_group(slot_rows, slot_prefix, w_query, w_key, w_value)
    mixed = attend_slots(
        packed, cache_keys, cache_values, slot_prefix, slot_length, q_width, kv_width
    )
    outgoing_back = jnp.einsum(
        "sj,csf->jcf", recv_table, mixed, preferred_element_type=jnp.float32
    ).astype(jnp.bfloat16)
    returned = lax.all_to_all(outgoing_back, "dp", split_axis=0, concat_axis=0, tiled=True)
    request_heads = jnp.einsum(
        "js,jcf->csf", send_table, returned, preferred_element_type=jnp.float32
    ).astype(jnp.bfloat16)
    span_rows = request_heads.shape[0]
    flat_heads = request_heads.reshape(span_rows * per_device, q_width)
    summed = lax.psum_scatter(
        jnp.dot(flat_heads, w_out, preferred_element_type=jnp.float32).astype(jnp.bfloat16),
        "tensor",
        scatter_dimension=0,
        tiled=True,
    ).astype(jnp.float32)
    return summed.reshape(hidden_rows.shape[0], per_device, -1).astype(jnp.bfloat16)


def solution(mesh):
    placed = (
        P("tensor", "dp", None),
        P(),
        P(None, "tensor"),
        P(None, "tensor"),
        P(None, "tensor"),
        P("tensor", None),
        P("dp", None, "tensor"),
        P("dp", None, "tensor"),
        P(),
        P(),
        P(),
    )
    return jax.shard_map(
        local, mesh=mesh, in_specs=placed, out_specs=P("tensor", "dp", None), check_vma=False
    )
```

profile of v0, /device:TPU:1, one launch (start us, length us, event | category | flops | bytes accessed | tf_op | source)
XLA Modules:
  0.0 441.6 jit_solution(15629852325169047121)
XLA Ops:
  6.5 0.0 copy-start
  6.5 2.6 fusion.16
  9.1 0.7 and_select_fusion
  9.8 7.6 %convolution_convert_fusion.1 = bf16[16,32,8192]{2,0,1:T(8,128)(2,1)} fusion(bf16[32,2,8192]{2,1,0:T(2,128)(2,1)} %param.11, f32[8192]{0:T(1024)} %param.12, f32[32,2]{1,0:T(8,128)S(1)} %add_rsqrt_fusion, s32[2]{0:T(128)S(1)} %and_select_fusion), kind=kOutput, calls=%fused_computation.6 | convolution fusion | flops 23068704 | bytes 9470216 | tf_op jit(solution)/shard_map/js,csf->jcf/dot_general | solution.py:136
  17.5 11.2 %copy.63 = bf16[16,32,8192]{2,1,0:T(8,128)(2,1)} copy(bf16[16,32,8192]{2,0,1:T(8,128)(2,1)} %convolution_convert_fusion.1) | data formatting | bytes 16777216 | tf_op jit(solution)/shard_map/convert_element_type | solution.py:138
  28.6 0.0 copy-start.4
  28.7 0.0 copy-start.5
  28.7 0.0 copy-start.6
  28.7 7.8 %all-to-all-start = ((bf16[16,32,8192]{2,1,0:T(8,128)(2,1)}), bf16[16,32,8192]{2,1,0:T(8,128)(2,1)}, u32[]{:S(2)}, u32[]{:S(2)}) async-start(bf16[16,32,8192]{2,1,0:T(8,128)(2,1)} %copy.63), calls=%async_computation | async-start | bytes 16777216 | tf_op jit(solution)/shard_map/all_to_all | solution.py:139
  36.4 0.2 all-gather.2.cloned.1.call-start
  36.7 0.0 copy-done.4
  36.7 0.0 copy-done.5
  36.7 0.0 copy-done.6
  36.7 0.2 select_reduce_fusion
  36.9 0.1 and_reduce_fusion
  37.0 145.5 %all-to-all-done = bf16[16,32,8192]{2,1,0:T(8,128)(2,1)} async-done(((bf16[16,32,8192]{2,1,0:T(8,128)(2,1)}), bf16[16,32,8192]{2,1,0:T(8,128)(2,1)}, u32[]{:S(2)}, u32[]{:S(2)}) %all-to-all-start) | async-done | bytes 8388640 | tf_op jit(solution)/shard_map/all_to_all | solution.py:139
  182.5 9.4 %fusion.3 = bf16[32,2,8192]{2,1,0:T(2,128)(2,1)} fusion(bf16[16,32,8192]{2,1,0:T(8,128)(2,1)} %all-to-all-done, pred[2,16]{1,0:T(4,128)(4,1)S(1)} %and_reduce_fusion), kind=kOutput, calls=%fused_computation.8 | convolution fusion | flops 17301504 | bytes 9437216 | tf_op jit(solution)/shard_map/sj,jcf->csf/dot_general | solution.py:140
  191.9 0.0 all-gather.2.cloned.1.call-update
  191.9 0.3 reduce-scatter.2.cloned.1.call-start
  192.3 0.1 iota_compare_fusion.3
  192.3 0.1 add_convert_fusion.1
  192.4 0.1 broadcast_and_fusion
  192.5 1.7 multiply_cosine_fusion
  194.3 0.1 iota_compare_fusion.1
  194.4 53.7 %all-gather.2.cloned.1.call-done = bf16[256,2,8192]{2,1,0:T(2,128)(2,1)} async-done(((bf16[32,2,8192]{2,1,0:T(2,128)(2,1)}), bf16[256,2,8192]{2,1,0:T(2,128)(2,1)}) %all-gather.2.cloned.1.call-update) | async-done | bytes 8388624 | tf_op jit(solution)/shard_map/all_gather | solution.py:35
  248.0 0.0 copy-start.7
  248.0 8.9 %fusion.38 = f32[256,2,1,128]{0,3,1,2:T(8,128)S(1)} fusion(bf16[8192,128]{1,0:T(8,128)(2,1)} %param.14, bf16[256,2,8192]{2,1,0:T(2,128)(2,1)} %all-gather.2.cloned.1.call-done), kind=kOutput, calls=%fused_computation.38 | convolution fusion | flops 1073741824 | bytes 10747904 | tf_op jit(solution)/shard_map/nsd,df->nsf/dot_general | solution.py:43
  256.9 1.2 fusion.78
  258.1 0.0 copy-done.7
  258.1 13.0 %fusion.6 = f32[256,2,512]{2,0,1:T(8,128)} fusion(bf16[8192,512]{1,0:T(8,128)(2,1)} %param.13, bf16[256,2,8192]{2,1,0:T(2,128)(2,1)S(1)} %copy-done.7), kind=kOutput, calls=%fused_computation.11 | convolution fusion | flops 4294967296 | bytes 17825792 | tf_op jit(solution)/shard_map/nsd,df->nsf/dot_general | solution.py:41
  271.1 1.6 reshape.282
  272.7 0.6 fusion.91
  273.3 1.2 subtract_convert_fusion
  274.5 0.0 copy-start.2
  274.5 0.0 copy-start.3
  274.5 9.1 %fusion.2 = (f32[2,4,256]{2,1,0:T(4,128)S(1)}, f32[2,256,4,2048]{3,1,2,0:T(8,128)}) fusion(pred[2,2048]{1,0:T(4,128)(4,1)S(1)} %iota_compare_fusion.1, bf16[2,2048,128]{2,1,0:T(8,128)(2,1)} %param.17, bf16[256,2,4,64]{3,0,2,1:T(8,128)(2,1)S(1)} %get-tuple-element.9, bf16[256,2,4,64]{3,0,2,1:T(8,128)(2,1)S(1)} %get-tuple-element.8), kind=kOutput, calls=%fused_computation.4 | convolution fusion | flops 1087371264 | bytes 18362368 | tf_op jit(solution)/shard_map/csgmd,spgd->sgmcp/dot_general | solution.py:71
  283.6 0.0 copy-done.2
  283.6 0.0 copy-done.3
  283.6 2.1 fusion.22
  285.8 0.0 copy-done
  285.8 0.0 copy-start.8
  285.8 14.5 %fusion.57 = f32[2,128,4,256]{3,1,2,0:T(8,128)} fusion(f32[2,256,256,4]{2,1,3,0:T(8,128)} %get-tuple-element.19, f32[2,4,256]{2,1,0:T(4,128)S(1)} %add.80, pred[2,256,256]{1,2,0:T(8,128)(4,1)S(1)} %broadcast_and_fusion, bf16[8192,128]{1,0:T(8,128)(2,1)S(1)} %copy-done, bf16[256,2,8192]{2,1,0:T(2,128)(2,1)} %all-gather.2.cloned.1.call-done), kind=kOutput, calls=%fused_computation.44 | convolution fusion | flops 1210122240 | bytes 13770752 | tf_op jit(solution)/shard_map/sgmcj,jsgd->csgmd/dot_general | solution.py:95
  300.3 0.0 copy-done.8
  300.3 8.0 %fusion.32 = bf16[2,128,4,256]{3,1,2,0:T(8,128)(2,1)S(1)} fusion(f32[2,128,4,256]{3,1,2,0:T(8,128)} %fusion.57, f32[2,4,256]{2,1,0:T(4,128)S(1)} %add.80, f32[2,256,4,2048]{3,1,2,0:T(8,128)} %get-tuple-element.17, pred[2,2048]{1,0:T(4,128)(4,1)S(1)} %iota_compare_fusion.1, bf16[2,2048,128]{2,1,0:T(8,128)(2,1)S(1)} %copy-done.8), kind=kOutput, calls=%fused_computation.36 | convolution fusion | flops 1091043328 | bytes 19410944 | tf_op jit(solution)/shard_map/sgmcp,spgd->csgmd/dot_general | solution.py:92
  308.3 0.5 copy.75
  308.8 1.6 convolution_convert_fusion.3
  310.5 2.4 copy.76
  312.9 56.0 %all_to_all.10 = bf16[16,256,512]{2,1,0:T(8,128)(2,1)S(1)} all-to-all(bf16[16,256,512]{2,1,0:T(8,128)(2,1)S(1)} %copy.76), channel_id=1, replica_groups=mesh['dp'=16,'tensor'=8] {'dp'}, dimensions={0} | all-to-all | bytes 8388608 | tf_op jit(solution)/shard_map/all_to_all | solution.py:150
  368.8 2.5 fusion.35
  371.4 0.2 reshape.287
  371.6 0.0 copy-start.1
  371.6 10.2 %convolution_convert_fusion = bf16[512,8192]{1,0:T(8,128)(2,1)} fusion(bf16[512,512]{1,0:T(8,128)(2,1)S(1)} %reshape.287, bf16[512,8192]{1,0:T(8,128)(2,1)} %param.16), kind=kOutput, calls=%fused_computation.5 | convolution fusion | flops 4299161600 | bytes 17301504 | tf_op jit(solution)/shard_map/dot_general | solution.py:157
  381.8 0.0 reduce-scatter.2.cloned.1.call-update
  381.8 50.2 %reduce-scatter.2.cloned.1.call-done = bf16[64,8192]{1,0:T(8,128)(2,1)} async-done(((bf16[512,8192]{1,0:T(8,128)(2,1)}), bf16[64,8192]{1,0:T(8,128)(2,1)}) %reduce-scatter.2.cloned.1.call-update) | async-done | bytes 1048592 | tf_op jit(solution)/shard_map/reduce_scatter | solution.py:156
  432.1 2.5 convert_element_type.82
  434.6 0.0 copy-done.1
  (7 shorter events, 0.1 us)
Async XLA Ops:
  6.5 279.2 %copy-start = (bf16[8192,128]{1,0:T(8,128)(2,1)S(1)}, bf16[8192,128]{1,0:T(8,128)(2,1)}, u32[]{:S(2)}) copy-start(bf16[8192,128]{1,0:T(8,128)(2,1)} %param.15) | copy-start | bytes 6291460
  28.6 8.0 %copy-start.4 = (s32[32]{0:T(128)S(1)}, s32[32]{0:T(128)}, u32[]{:S(2)}) copy-start(s32[32]{0:T(128)} %param.19) | copy-start | bytes 388
  28.7 8.0 %copy-start.5 = (s32[32]{0:T(128)S(1)}, s32[32]{0:T(128)}, u32[]{:S(2)}) copy-start(s32[32]{0:T(128)} %param.20) | copy-start | bytes 388
  28.7 8.1 %copy-start.6 = (s32[32]{0:T(128)S(1)}, s32[32]{0:T(128)}, u32[]{:S(2)}) copy-start(s32[32]{0:T(128)} %param.21) | copy-start | bytes 388
  28.7 153.8 %all-to-all-start = ((bf16[16,32,8192]{2,1,0:T(8,128)(2,1)}), bf16[16,32,8192]{2,1,0:T(8,128)(2,1)}, u32[]{:S(2)}, u32[]{:S(2)}) async-start(bf16[16,32,8192]{2,1,0:T(8,128)(2,1)} %copy.63), calls=%async_computation | async-start | bytes 16777216 | tf_op jit(solution)/shard_map/all_to_all | solution.py:139
  36.4 211.6 %all-gather.2.cloned.1.call-start = ((), (), s32[]{:S(2)}) async-start(), calls=%async_computation.3 | async-start | bytes 9437184 | tf_op jit(solution)/shard_map/all_gather | solution.py:35
  191.9 240.1 %reduce-scatter.2.cloned.1.call-start = ((), (), s32[]{:S(2)}) async-start(), calls=%async_computation.4 | async-start | bytes 9437184 | tf_op jit(solution)/shard_map/reduce_scatter | solution.py:156
  248.0 10.1 %copy-start.7 = (bf16[256,2,8192]{2,1,0:T(2,128)(2,1)S(1)}, bf16[256,2,8192]{2,1,0:T(2,128)(2,1)}, u32[]{:S(2)}) copy-start(bf16[256,2,8192]{2,1,0:T(2,128)(2,1)} %all-gather.2.cloned.1.call-done) | copy-start | bytes 25165828
  274.5 9.1 %copy-start.2 = (bf16[256,2,64]{0,2,1:T(8,128)(2,1)S(1)}, bf16[256,2,64]{0,2,1:T(8,128)(2,1)}, u32[]{:S(2)}) copy-start(bf16[256,2,64]{0,2,1:T(8,128)(2,1)} %get-tuple-element.12) | copy-start | bytes 196612
  274.5 9.1 %copy-start.3 = (bf16[256,2,64]{0,2,1:T(8,128)(2,1)S(1)}, bf16[256,2,64]{0,2,1:T(8,128)(2,1)}, u32[]{:S(2)}) copy-start(bf16[256,2,64]{0,2,1:T(8,128)(2,1)} %get-tuple-element.13) | copy-start | bytes 196612
  285.8 14.5 %copy-start.8 = (bf16[2,2048,128]{2,1,0:T(8,128)(2,1)S(1)}, bf16[2,2048,128]{2,1,0:T(8,128)(2,1)}, u32[]{:S(2)}) copy-start(bf16[2,2048,128]{2,1,0:T(8,128)(2,1)} %param.18) | copy-start | bytes 3145732
  371.6 63.0 %copy-start.1 = (bf16[8192,128]{1,0:T(8,128)(2,1)S(1)}, bf16[8192,128]{1,0:T(8,128)(2,1)}, u32[]{:S(2)}) copy-start(bf16[8192,128]{1,0:T(8,128)(2,1)} %param.15) | copy-start | bytes 6291460
Sparse Core Ops, SparseCore 0:
  192.1 55.9 all-gather.1
  382.0 50.0 reduce-scatter.1
where the time goes:
time: 448 us; the launch traced here: 442 us
  waiting for transfers between devices  249 us (56%)
  matrix products  87 us (19%)
  blocking collectives  56 us (12%)
  local copies, waits for them, and re-layouts  19 us (4%)
  between operations  13.8 us (3%)
  starting transfers between devices  8.23 us (2%)
  other arithmetic  8.21 us (2%)
    all_to_all x1, waiting for transfers between devices, local(): lax.all_to_all(outgoing, 'dp', split_axis=0, concat_axis=0, tiled=True)  145 us
    all_to_all x1, blocking collectives, local(): lax.all_to_all(outgoing_back, 'dp', split_axis=0, concat_axis=0, tiled=True)  56 us
    all_gather x1, waiting for transfers between devices, project_group(): piece_rows = lax.all_gather(normed, 'tensor', axis=0, tiled=True)  53.7 us
    reduce_scatter x1, waiting for transfers between devices, local(): lax.psum_scatter(jnp.dot(flat_heads, w_out, preferred_element_type=jnp.fl...  50.2 us
    dot_general x1, matrix products, attend_slots(): jnp.einsum('sgmcj,jsgd->csgmd', weight_new, values_new, preferred_element...  14.5 us
    dot_general x1, matrix products, project_group(): jnp.einsum('nsd,df->nsf', piece_rows, w_query, preferred_element_type=jnp...  13 us
    convert_element_type x1, local copies, waits for them, and re-layouts, local(): outgoing = jnp.einsum('js,csf->jcf', send_table, normed, preferred_elemen...  11.2 us
    dot_general x1, matrix products, local(): jnp.dot(flat_heads, w_out, preferred_element_type=jnp.float32)  10.2 us
  transfers between devices with their start and end apart: 3, of which 3 were waited for; matrix products, arithmetic and copies ran while one was open for 1% of the time, Pallas kernels for 0%

commit v1 on v0

--- a/solution.py
+++ b/solution.py
@@ -32,7 +32,14 @@
 
 
 def project_group(normed, prefix_here, w_query, w_key, w_value):
-    piece_rows = lax.all_gather(normed, "tensor", axis=0, tiled=True)
+    ring = [normed]
+    for hop in range(7):
+        ring.append(lax.ppermute(ring[-1], "tensor", [(dev, (dev + 1) % 8) for dev in range(8)]))
+    piece_rows = jnp.roll(
+        jnp.concatenate(ring[::-1], axis=0),
+        (lax.axis_index("tensor") + 1) * ring[0].shape[0],
+        axis=0,
+    )
     row_count = piece_rows.shape[0]
     request_count = piece_rows.shape[1]
     positions = (prefix_here[None, :] + jnp.arange(row_count, dtype=jnp.int32)[:, None]).astype(

time: 448 us -> 537 us (1.20)
  local copies, waits for them, and re-layouts: 19 us -> 59.7 us
  waiting for transfers between devices: 249 us -> 289 us
  starting transfers between devices: 8.23 us -> 27.1 us
  blocking collectives: 56 us -> 47.8 us
    ppermute x0 -> x7, waiting for transfers between devices: none -> 79.8 us  [project_group(): lax.ppermute(ring[-1], 'tensor', [(dev, (dev + 1) % 8) for dev in range(8)])]
    all_gather x1 -> x0, waiting for transfers between devices: 53.7 us -> none  [project_group(): piece_rows = lax.all_gather(normed, 'tensor', axis=0, tiled=True)]
    unnamed x18 -> x65, local copies, waits for them, and re-layouts: 0.04 us -> 33.2 us
    ppermute x0 -> x7, starting transfers between devices: none -> 19.1 us  [project_group(): lax.ppermute(ring[-1], 'tensor', [(dev, (dev + 1) % 8) for dev in range(8)])]
    reduce_scatter x1, waiting for transfers between devices: 50.2 us -> 64.1 us  [local(): lax.psum_scatter(jnp.dot(flat_heads, w_out, preferred_element_type=jnp.fl...]
    all_to_all x1, blocking collectives: 56 us -> 47.8 us  [local(): lax.all_to_all(outgoing_back, 'dp', split_axis=0, concat_axis=0, tiled=True)]
    dynamic_slice x0 -> x1, local copies, waits for them, and re-layouts: none -> 6.53 us  [project_group(): jnp.roll(jnp.concatenate(ring[::-1], axis=0), (lax.axis_index('tensor') +...]
  transfers between devices with their start and end apart: 3 -> 9, of which waited for: 3 -> 9; matrix products, arithmetic and copies ran while one was open for 1% -> 1% of each run, Pallas kernels for 0% -> 0%
where the time goes in v1:
time: 537 us; the launch traced here: 530 us
  waiting for transfers between devices  289 us (54%)
  matrix products  84.7 us (16%)
  local copies, waits for them, and re-layouts  59.7 us (11%)
  blocking collectives  47.8 us (9%)
  starting transfers between devices  27.1 us (5%)
  between operations  14.4 us (3%)
  other arithmetic  6.84 us (1%)
    all_to_all x1, waiting for transfers between devices, local(): lax.all_to_all(outgoing, 'dp', split_axis=0, concat_axis=0, tiled=True)  145 us
    ppermute x7, waiting for transfers between devices, project_group(): lax.ppermute(ring[-1], 'tensor', [(dev, (dev + 1) % 8) for dev in range(8)])  79.8 us
    reduce_scatter x1, waiting for transfers between devices, local(): lax.psum_scatter(jnp.dot(flat_heads, w_out, preferred_element_type=jnp.fl...  64.1 us
    all_to_all x1, blocking collectives, local(): lax.all_to_all(outgoing_back, 'dp', split_axis=0, concat_axis=0, tiled=True)  47.8 us
    unnamed x65, local copies, waits for them, and re-layouts  33.2 us
    ppermute x7, starting transfers between devices, project_group(): lax.ppermute(ring[-1], 'tensor', [(dev, (dev + 1) % 8) for dev in range(8)])  19.1 us
    dot_general x1, matrix products, attend_slots(): jnp.einsum('sgmcj,jsgd->csgmd', weight_new, values_new, preferred_element...  14.5 us
    dot_general x1, matrix products, project_group(): jnp.einsum('nsd,df->nsf', piece_rows, w_query, preferred_element_type=jnp...  12.9 us
  transfers between devices with their start and end apart: 9, of which 9 were waited for; matrix products, arithmetic and copies ran while one was open for 1% of the time, Pallas kernels for 0%

profile of v1, /device:TPU:1, one launch (start us, length us, event | category | flops | bytes accessed | tf_op | source)
XLA Modules:
  0.0 529.8 jit_solution(2248412847715884853)
XLA Ops:
  6.5 2.6 fusion.16
  9.1 0.7 and_select_fusion
  9.8 0.5 copy-done.18
  10.4 7.6 %convolution_convert_fusion.1 = bf16[16,32,8192]{2,0,1:T(8,128)(2,1)} fusion(bf16[32,2,8192]{2,1,0:T(2,128)(2,1)} %param.11, f32[8192]{0:T(1024)} %param.12, f32[32,2]{1,0:T(8,128)S(1)} %add_rsqrt_fusion, s32[2]{0:T(128)S(1)} %and_select_fusion), kind=kOutput, calls=%fused_computation.6 | convolution fusion | flops 23068704 | bytes 9470216 | tf_op jit(solution)/shard_map/js,csf->jcf/dot_general | solution.py:143
  18.0 11.2 %copy.63 = bf16[16,32,8192]{2,1,0:T(8,128)(2,1)} copy(bf16[16,32,8192]{2,0,1:T(8,128)(2,1)} %convolution_convert_fusion.1) | data formatting | bytes 16777216 | tf_op jit(solution)/shard_map/convert_element_type | solution.py:145
  29.2 7.8 %all-to-all-start = ((bf16[16,32,8192]{2,1,0:T(8,128)(2,1)}), bf16[16,32,8192]{2,1,0:T(8,128)(2,1)}, u32[]{:S(2)}, u32[]{:S(2)}) async-start(bf16[16,32,8192]{2,1,0:T(8,128)(2,1)} %copy.63), calls=%async_computation | async-start | bytes 16777216 | tf_op jit(solution)/shard_map/all_to_all | solution.py:146
  37.6 145.4 %all-to-all-done = bf16[16,32,8192]{2,1,0:T(8,128)(2,1)} async-done(((bf16[16,32,8192]{2,1,0:T(8,128)(2,1)}), bf16[16,32,8192]{2,1,0:T(8,128)(2,1)}, u32[]{:S(2)}, u32[]{:S(2)}) %all-to-all-start) | async-done | bytes 8388640 | tf_op jit(solution)/shard_map/all_to_all | solution.py:146
  183.0 8.5 %fusion.3 = bf16[32,2,8192]{2,1,0:T(2,128)(2,1)S(1)} fusion(bf16[16,32,8192]{2,1,0:T(8,128)(2,1)} %all-to-all-done, pred[2,16]{1,0:T(4,128)(4,1)S(1)} %and_reduce_fusion), kind=kOutput, calls=%fused_computation.8 | convolution fusion | flops 17301504 | bytes 9437216 | tf_op jit(solution)/shard_map/sj,jcf->csf/dot_general | solution.py:147
  191.5 4.1 collective-permute-start
  195.6 11.7 %collective-permute-done = bf16[32,2,8192]{2,1,0:T(2,128)(2,1)S(1)} collective-permute-done((bf16[32,2,8192]{2,1,0:T(2,128)(2,1)S(1)}, bf16[32,2,8192]{2,1,0:T(2,128)(2,1)S(1)}, u32[]{:S(2)}, u32[]{:S(2)}) %collective-permute-start) | collective-permute-done | bytes 1048608 | tf_op jit(solution)/shard_map/ppermute | solution.py:37
  207.4 1.0 copy-done.3
  208.3 2.5 collective-permute-start.1
  210.8 11.7 %collective-permute-done.1 = bf16[32,2,8192]{2,1,0:T(2,128)(2,1)S(1)} collective-permute-done((bf16[32,2,8192]{2,1,0:T(2,128)(2,1)S(1)}, bf16[32,2,8192]{2,1,0:T(2,128)(2,1)S(1)}, u32[]{:S(2)}, u32[]{:S(2)}) %collective-permute-start.1) | collective-permute-done | bytes 1048608 | tf_op jit(solution)/shard_map/ppermute | solution.py:37
  222.6 1.0 copy-done.5
  223.5 2.5 collective-permute-start.2
  226.0 11.7 %collective-permute-done.2 = bf16[32,2,8192]{2,1,0:T(2,128)(2,1)S(1)} collective-permute-done((bf16[32,2,8192]{2,1,0:T(2,128)(2,1)S(1)}, bf16[32,2,8192]{2,1,0:T(2,128)(2,1)S(1)}, u32[]{:S(2)}, u32[]{:S(2)}) %collective-permute-start.2) | collective-permute-done | bytes 1048608 | tf_op jit(solution)/shard_map/ppermute | solution.py:37
  237.7 1.0 copy-done.7
  238.7 2.5 collective-permute-start.3
  241.2 11.7 %collective-permute-done.3 = bf16[32,2,8192]{2,1,0:T(2,128)(2,1)S(1)} collective-permute-done((bf16[32,2,8192]{2,1,0:T(2,128)(2,1)S(1)}, bf16[32,2,8192]{2,1,0:T(2,128)(2,1)S(1)}, u32[]{:S(2)}, u32[]{:S(2)}) %collective-permute-start.3) | collective-permute-done | bytes 1048608 | tf_op jit(solution)/shard_map/ppermute | solution.py:37
  253.0 1.0 copy-done.9
  253.9 2.5 collective-permute-start.4
  256.4 11.7 %collective-permute-done.4 = bf16[32,2,8192]{2,1,0:T(2,128)(2,1)S(1)} collective-permute-done((bf16[32,2,8192]{2,1,0:T(2,128)(2,1)S(1)}, bf16[32,2,8192]{2,1,0:T(2,128)(2,1)S(1)}, u32[]{:S(2)}, u32[]{:S(2)}) %collective-permute-start.4) | collective-permute-done | bytes 1048608 | tf_op jit(solution)/shard_map/ppermute | solution.py:37
  268.2 1.0 copy-done.11
  269.1 2.5 collective-permute-start.5
  271.8 11.6 %collective-permute-done.5 = bf16[32,2,8192]{2,1,0:T(2,128)(2,1)} collective-permute-done((bf16[32,2,8192]{2,1,0:T(2,128)(2,1)S(1)}, bf16[32,2,8192]{2,1,0:T(2,128)(2,1)}, u32[]{:S(2)}, u32[]{:S(2)}) %collective-permute-start.5) | collective-permute-done | bytes 1048608 | tf_op jit(solution)/shard_map/ppermute | solution.py:37
  283.4 2.6 collective-permute-start.6
  286.5 2.0 multiply_cosine_fusion
  288.5 9.5 %collective-permute-done.6 = bf16[32,2,8192]{2,1,0:T(2,128)(2,1)} collective-permute-done((bf16[32,2,8192]{2,1,0:T(2,128)(2,1)}, bf16[32,2,8192]{2,1,0:T(2,128)(2,1)}, u32[]{:S(2)}, u32[]{:S(2)}) %collective-permute-start.6) | collective-permute-done | bytes 1048608 | tf_op jit(solution)/shard_map/ppermute | solution.py:37
  298.0 2.1 constant_dynamic-update-slice_fusion.15
  300.1 2.5 constant_dynamic-update-slice_fusion.14
  302.6 2.6 constant_dynamic-update-slice_fusion.13
  305.3 2.6 constant_dynamic-update-slice_fusion.12
  307.9 1.0 constant_dynamic-update-slice_fusion.11
  308.9 1.0 constant_dynamic-update-slice_fusion.10
  309.9 1.0 constant_dynamic-update-slice_fusion.9
  310.9 1.0 constant_dynamic-update-slice_fusion.8
  311.9 2.5 constant_dynamic-update-slice_fusion.7
  314.4 2.5 constant_dynamic-update-slice_fusion.6
  317.0 1.0 constant_dynamic-update-slice_fusion.5
  318.0 1.0 constant_dynamic-update-slice_fusion.4
  319.0 1.0 constant_dynamic-update-slice_fusion.3
  319.9 1.0 constant_dynamic-update-slice_fusion.2
  320.9 1.4 constant_dynamic-update-slice_fusion.1
  322.4 1.0 constant_dynamic-update-slice_fusion
  323.3 6.5 %constant_dynamic-slice_fusion = bf16[256,2,8192]{2,1,0:T(2,128)(2,1)S(1)} fusion(bf16[512,2,8192]{2,1,0:T(2,128)(2,1)S(1)} %constant_dynamic-update-slice_fusion, s32[]{:T(128)S(6)} %select_n.53), kind=kLoop, calls=%fused_computation.114 | loop fusion | bytes 16777220 | tf_op jit(solution)/shard_map/jit(_roll_dynamic)/dynamic_slice | solution.py:38
  329.9 3.2 copy-done.2
  333.1 12.9 %fusion.6 = f32[256,2,512]{2,0,1:T(8,128)} fusion(bf16[8192,512]{1,0:T(8,128)(2,1)} %param.13, bf16[256,2,8192]{2,1,0:T(2,128)(2,1)S(1)} %constant_dynamic-slice_fusion), kind=kOutput, calls=%fused_computation.11 | convolution fusion | flops 4294967296 | bytes 17825792 | tf_op jit(solution)/shard_map/nsd,df->nsf/dot_general | solution.py:48
  346.1 1.6 reshape.282
  347.6 0.6 fusion.91
  348.3 8.7 %fusion.38 = f32[256,2,1,128]{0,3,1,2:T(8,128)S(1)} fusion(bf16[8192,128]{1,0:T(8,128)(2,1)} %param.14, bf16[256,2,8192]{2,1,0:T(2,128)(2,1)} %copy-done.2), kind=kOutput, calls=%fused_computation.38 | convolution fusion | flops 1073741824 | bytes 10747904 | tf_op jit(solution)/shard_map/nsd,df->nsf/dot_general | solution.py:50
  357.0 0.6 fusion.78
  357.6 0.3 subtract_convert_fusion
  357.9 7.8 %fusion.2 = (f32[2,4,256]{2,1,0:T(4,128)S(1)}, f32[2,256,4,2048]{3,1,2,0:T(8,128)}) fusion(pred[2,2048]{1,0:T(4,128)(4,1)S(1)} %iota_compare_fusion.1, bf16[2,2048,128]{2,1,0:T(8,128)(2,1)S(1)} %copy-done.23, bf16[256,2,4,64]{3,0,2,1:T(8,128)(2,1)S(1)} %get-tuple-element.9, bf16[256,2,4,64]{3,0,2,1:T(8,128)(2,1)S(1)} %get-tuple-element.8), kind=kOutput, calls=%fused_computation.4 | convolution fusion | flops 1087371264 | bytes 18362368 | tf_op jit(solution)/shard_map/csgmd,spgd->sgmcp/dot_general | solution.py:78
  365.7 2.2 fusion.22
  367.9 14.5 %fusion.57 = f32[2,128,4,256]{3,1,2,0:T(8,128)} fusion(f32[2,256,256,4]{2,1,3,0:T(8,128)} %get-tuple-element.19, f32[2,4,256]{2,1,0:T(4,128)S(1)} %add.96, pred[2,256,256]{1,2,0:T(8,128)(4,1)S(1)} %broadcast_and_fusion, bf16[8192,128]{1,0:T(8,128)(2,1)S(1)} %copy-done, bf16[256,2,8192]{2,1,0:T(2,128)(2,1)} %copy-done.2), kind=kOutput, calls=%fused_computation.44 | convolution fusion | flops 1210122240 | bytes 13770752 | tf_op jit(solution)/shard_map/sgmcj,jsgd->csgmd/dot_general | solution.py:102
  382.4 8.1 %fusion.32 = bf16[2,128,4,256]{3,1,2,0:T(8,128)(2,1)S(1)} fusion(f32[2,128,4,256]{3,1,2,0:T(8,128)} %fusion.57, f32[2,4,256]{2,1,0:T(4,128)S(1)} %add.96, f32[2,256,4,2048]{3,1,2,0:T(8,128)} %get-tuple-element.17, pred[2,2048]{1,0:T(4,128)(4,1)S(1)} %iota_compare_fusion.1, bf16[2,2048,128]{2,1,0:T(8,128)(2,1)S(1)} %copy-done.24), kind=kOutput, calls=%fused_computation.36 | convolution fusion | flops 1091043328 | bytes 19410944 | tf_op jit(solution)/shard_map/sgmcp,spgd->csgmd/dot_general | solution.py:99
  390.6 0.5 copy.75
  391.1 1.6 convolution_convert_fusion.3
  392.7 2.4 copy.76
  395.1 47.8 %all_to_all.10 = bf16[16,256,512]{2,1,0:T(8,128)(2,1)S(1)} all-to-all(bf16[16,256,512]{2,1,0:T(8,128)(2,1)S(1)} %copy.76), channel_id=1, replica_groups=mesh['dp'=16,'tensor'=8] {'dp'}, dimensions={0} | all-to-all | bytes 8388608 | tf_op jit(solution)/shard_map/all_to_all | solution.py:157
  442.9 2.5 fusion.35
  445.7 10.3 %convolution_convert_fusion = bf16[512,8192]{1,0:T(8,128)(2,1)} fusion(bf16[512,512]{1,0:T(8,128)(2,1)S(1)} %reshape.287, bf16[512,8192]{1,0:T(8,128)(2,1)} %param.16), kind=kOutput, calls=%fused_computation.5 | convolution fusion | flops 4299161600 | bytes 17301504 | tf_op jit(solution)/shard_map/dot_general | solution.py:164
  455.9 64.1 %reduce-scatter.2.cloned.1.call-done = bf16[64,8192]{1,0:T(8,128)(2,1)} async-done(((bf16[512,8192]{1,0:T(8,128)(2,1)}), bf16[64,8192]{1,0:T(8,128)(2,1)}) %reduce-scatter.2.cloned.1.call-update) | async-done | bytes 1048592 | tf_op jit(solution)/shard_map/reduce_scatter | solution.py:163
  520.0 2.5 convert_element_type.82
  (59 shorter events, 1.6 us)
Async XLA Ops:
  6.5 361.4 %copy-start = (bf16[8192,128]{1,0:T(8,128)(2,1)S(1)}, bf16[8192,128]{1,0:T(8,128)(2,1)}, u32[]{:S(2)}) copy-start(bf16[8192,128]{1,0:T(8,128)(2,1)} %param.15) | copy-start | bytes 6291460
  9.8 0.5 copy-start.18
  29.2 8.1 %copy-start.20 = (s32[32]{0:T(128)S(1)}, s32[32]{0:T(128)}, u32[]{:S(2)}) copy-start(s32[32]{0:T(128)} %param.20) | copy-start | bytes 388
  29.2 8.1 %copy-start.21 = (s32[32]{0:T(128)S(1)}, s32[32]{0:T(128)}, u32[]{:S(2)}) copy-start(s32[32]{0:T(128)} %param.21) | copy-start | bytes 388
  29.2 8.1 %copy-start.22 = (s32[32]{0:T(128)S(1)}, s32[32]{0:T(128)}, u32[]{:S(2)}) copy-start(s32[32]{0:T(128)} %param.19) | copy-start | bytes 388
  29.2 153.8 %all-to-all-start = ((bf16[16,32,8192]{2,1,0:T(8,128)(2,1)}), bf16[16,32,8192]{2,1,0:T(8,128)(2,1)}, u32[]{:S(2)}, u32[]{:S(2)}) async-start(bf16[16,32,8192]{2,1,0:T(8,128)(2,1)} %copy.63), calls=%async_computation | async-start | bytes 16777216 | tf_op jit(solution)/shard_map/all_to_all | solution.py:146
  37.0 483.0 %reduce-scatter.2.cloned.1.call-start = ((), (), s32[]{:S(2)}) async-start(), calls=%async_computation.3 | async-start | bytes 9437184 | tf_op jit(solution)/shard_map/reduce_scatter | solution.py:163
  37.6 153.9 %copy-start.16 = (pred[2,16]{1,0:T(4,128)(4,1)}, pred[2,16]{1,0:T(4,128)(4,1)S(1)}, u32[]{:S(2)}) copy-start(pred[2,16]{1,0:T(4,128)(4,1)S(1)} %and_reduce_fusion) | copy-start | bytes 100
  191.5 15.8 %collective-permute-start = (bf16[32,2,8192]{2,1,0:T(2,128)(2,1)S(1)}, bf16[32,2,8192]{2,1,0:T(2,128)(2,1)S(1)}, u32[]{:S(2)}, u32[]{:S(2)}) collective-permute-start(bf16[32,2,8192]{2,1,0:T(2,128)(2,1)S(1)} %fusion.3), channel_id=1, source_target_pairs={{0,1},{1,2},{2,3},{3,4},{4,5},{5,6},{6,7},{7,0},{8,9},{9,10},{10,1... | collective-permute-start | bytes 3145736 | tf_op jit(solution)/shard_map/ppermute | solution.py:37
  207.4 1.0 copy-start.3
  208.3 14.2 %collective-permute-start.1 = (bf16[32,2,8192]{2,1,0:T(2,128)(2,1)S(1)}, bf16[32,2,8192]{2,1,0:T(2,128)(2,1)S(1)}, u32[]{:S(2)}, u32[]{:S(2)}) collective-permute-start(bf16[32,2,8192]{2,1,0:T(2,128)(2,1)S(1)} %collective-permute-done), channel_id=1, source_target_pairs={{0,1},{1,2},{2,3},{3,4},{4,5},{5,6},{6,7},{7,0},{8,9},{9,10},{10,1... | collective-permute-start | bytes 3145736 | tf_op jit(solution)/shard_map/ppermute | solution.py:37
  222.6 1.0 copy-start.5
  223.5 14.2 %collective-permute-start.2 = (bf16[32,2,8192]{2,1,0:T(2,128)(2,1)S(1)}, bf16[32,2,8192]{2,1,0:T(2,128)(2,1)S(1)}, u32[]{:S(2)}, u32[]{:S(2)}) collective-permute-start(bf16[32,2,8192]{2,1,0:T(2,128)(2,1)S(1)} %collective-permute-done.1), channel_id=1, source_target_pairs={{0,1},{1,2},{2,3},{3,4},{4,5},{5,6},{6,7},{7,0},{8,9},{9,10},{10,1... | collective-permute-start | bytes 3145736 | tf_op jit(solution)/shard_map/ppermute | solution.py:37
  237.7 1.0 copy-start.7
  238.7 14.2 %collective-permute-start.3 = (bf16[32,2,8192]{2,1,0:T(2,128)(2,1)S(1)}, bf16[32,2,8192]{2,1,0:T(2,128)(2,1)S(1)}, u32[]{:S(2)}, u32[]{:S(2)}) collective-permute-start(bf16[32,2,8192]{2,1,0:T(2,128)(2,1)S(1)} %collective-permute-done.2), channel_id=1, source_target_pairs={{0,1},{1,2},{2,3},{3,4},{4,5},{5,6},{6,7},{7,0},{8,9},{9,10},{10,1... | collective-permute-start | bytes 3145736 | tf_op jit(solution)/shard_map/ppermute | solution.py:37
  253.0 1.0 copy-start.9
  253.9 14.2 %collective-permute-start.4 = (bf16[32,2,8192]{2,1,0:T(2,128)(2,1)S(1)}, bf16[32,2,8192]{2,1,0:T(2,128)(2,1)S(1)}, u32[]{:S(2)}, u32[]{:S(2)}) collective-permute-start(bf16[32,2,8192]{2,1,0:T(2,128)(2,1)S(1)} %collective-permute-done.3), channel_id=1, source_target_pairs={{0,1},{1,2},{2,3},{3,4},{4,5},{5,6},{6,7},{7,0},{8,9},{9,10},{10,1... | collective-permute-start | bytes 3145736 | tf_op jit(solution)/shard_map/ppermute | solution.py:37
  268.2 1.0 copy-start.11
  269.1 14.2 %collective-permute-start.5 = (bf16[32,2,8192]{2,1,0:T(2,128)(2,1)S(1)}, bf16[32,2,8192]{2,1,0:T(2,128)(2,1)}, u32[]{:S(2)}, u32[]{:S(2)}) collective-permute-start(bf16[32,2,8192]{2,1,0:T(2,128)(2,1)S(1)} %collective-permute-done.4), channel_id=1, source_target_pairs={{0,1},{1,2},{2,3},{3,4},{4,5},{5,6},{6,7},{7,0},{8,9},{9,10},{10,1... | collective-permute-start | bytes 3145736 | tf_op jit(solution)/shard_map/ppermute | solution.py:37
  283.4 14.6 %collective-permute-start.6 = (bf16[32,2,8192]{2,1,0:T(2,128)(2,1)}, bf16[32,2,8192]{2,1,0:T(2,128)(2,1)}, u32[]{:S(2)}, u32[]{:S(2)}) collective-permute-start(bf16[32,2,8192]{2,1,0:T(2,128)(2,1)} %collective-permute-done.5), channel_id=1, source_target_pairs={{0,1},{1,2},{2,3},{3,4},{4,5},{5,6},{6,7},{7,0},{8,9},{9,10},{10,1... | collective-permute-start | bytes 3145736 | tf_op jit(solution)/shard_map/ppermute | solution.py:37
  286.0 0.5 copy-start.14
  286.0 22.0 %copy-start.8 = (bf16[32,2,8192]{2,1,0:T(2,128)(2,1)S(1)}, bf16[32,2,8192]{2,1,0:T(2,128)(2,1)}, u32[]{:S(2)}) copy-start(bf16[32,2,8192]{2,1,0:T(2,128)(2,1)} %copy-done.7) | copy-start | bytes 3145732
  286.0 22.9 %copy-start.6 = (bf16[32,2,8192]{2,1,0:T(2,128)(2,1)S(1)}, bf16[32,2,8192]{2,1,0:T(2,128)(2,1)}, u32[]{:S(2)}) copy-start(bf16[32,2,8192]{2,1,0:T(2,128)(2,1)} %copy-done.5) | copy-start | bytes 3145732
  286.0 23.9 %copy-start.4 = (bf16[32,2,8192]{2,1,0:T(2,128)(2,1)S(1)}, bf16[32,2,8192]{2,1,0:T(2,128)(2,1)}, u32[]{:S(2)}) copy-start(bf16[32,2,8192]{2,1,0:T(2,128)(2,1)} %copy-done.3) | copy-start | bytes 3145732
  302.6 14.4 %copy-start.12 = (bf16[32,2,8192]{2,1,0:T(2,128)(2,1)S(1)}, bf16[32,2,8192]{2,1,0:T(2,128)(2,1)}, u32[]{:S(2)}) copy-start(bf16[32,2,8192]{2,1,0:T(2,128)(2,1)} %copy-done.11) | copy-start | bytes 3145732
  305.3 12.7 %copy-start.10 = (bf16[32,2,8192]{2,1,0:T(2,128)(2,1)S(1)}, bf16[32,2,8192]{2,1,0:T(2,128)(2,1)}, u32[]{:S(2)}) copy-start(bf16[32,2,8192]{2,1,0:T(2,128)(2,1)} %copy-done.9) | copy-start | bytes 3145732
  329.9 3.3 copy-start.2
  347.6 9.4 %copy-start.15 = (f32[64]{0:T(128)S(1)}, f32[64]{0:T(128)}, u32[]{:S(2)}) copy-start(f32[64]{0:T(128)} %copy-done.14) | copy-start | bytes 772
  347.6 10.0 %copy-start.13 = (f32[256,2,64]{2,0,1:T(8,128)S(1)}, f32[256,2,64]{2,0,1:T(8,128)}, u32[]{:S(2)}) copy-start(f32[256,2,64]{2,0,1:T(8,128)} %get-tuple-element.15) | copy-start | bytes 393220
  348.3 9.7 %copy-start.23 = (bf16[2,2048,128]{2,1,0:T(8,128)(2,1)S(1)}, bf16[2,2048,128]{2,1,0:T(8,128)(2,1)}, u32[]{:S(2)}) copy-start(bf16[2,2048,128]{2,1,0:T(8,128)(2,1)} %param.17) | copy-start | bytes 3145732
  367.9 14.5 %copy-start.24 = (bf16[2,2048,128]{2,1,0:T(8,128)(2,1)S(1)}, bf16[2,2048,128]{2,1,0:T(8,128)(2,1)}, u32[]{:S(2)}) copy-start(bf16[2,2048,128]{2,1,0:T(8,128)(2,1)} %param.18) | copy-start | bytes 3145732
  382.4 8.7 %copy-start.17 = (pred[2,16]{1,0:T(4,128)(4,1)S(1)}, pred[2,16]{1,0:T(4,128)(4,1)}, u32[]{:S(2)}) copy-start(pred[2,16]{1,0:T(4,128)(4,1)} %copy-done.16) | copy-start | bytes 100
  392.7 50.2 %copy-start.19 = (s32[2]{0:T(128)S(1)}, s32[2]{0:T(128)}, u32[]{:S(2)}) copy-start(s32[2]{0:T(128)} %copy-done.18) | copy-start | bytes 28
  445.6 76.9 %copy-start.1 = (bf16[8192,128]{1,0:T(8,128)(2,1)S(1)}, bf16[8192,128]{1,0:T(8,128)(2,1)}, u32[]{:S(2)}) copy-start(bf16[8192,128]{1,0:T(8,128)(2,1)} %param.15) | copy-start | bytes 6291460
Sparse Core Ops, SparseCore 0:
  456.1 63.8 reduce-scatter.1
